TPU v7x, 128 devices: a whole 4x4x4 slice. The times are simulated.
128 devices in a mesh: radar: 8 (over x, core), tile: 16 (over y, z).
Axes of the slice: x: 4, y: 4, z: 4, core: 2. Of those that a mesh axis runs over, the one named last changes fastest.
Arguments:
- background: float32 [3, 256, 32, 2048], P(None, 'tile', None, 'radar'), may hold values from -6 to 6
- interp: bfloat16 [32768, 128, 128], P(('radar', 'tile')), may hold values from -0.5 to 0.5
- beam: bfloat16 [32768, 3, 128], P(('radar', 'tile')), may hold values from -1 to 1
- observed: bfloat16 [32768, 128], P(('radar', 'tile')), may hold values from -6 to 6
- cell_block: int32 [32768], P(('radar', 'tile')), may hold values from 0 to 1023
- sweep_count: int32 [128, 128], P(('radar', 'tile')), may hold values from 0 to 2, as said below
Outputs:
- wind_field: float32 [3, 256, 32, 2048], P(None, 'tile', None, 'radar')
- strain: float32 [6, 256, 32, 2048], P(None, 'tile', None, 'radar')
- cost_trace: float32 [2], replicated
Inputs may be any that keep to these rules, and one draw needn't show every extreme that they name: `cell_block`: the cell block, within the owner's 16 x 32 x 256 cells of one component, read by a slot. `sweep_count`: every source device has an owning device to which all 2 of its slots are live.
All inputs are finite; a program needn't handle non-finite values.
Results may differ from a plain program's by a relative error of at most 0.0014.
Values may be sent and summed in bfloat16 or wider, within the bound.
A program may use at most 64 MiB of HBM per device.

v0:
```python
import jax
import jax.numpy as jnp
from jax import lax
from jax.sharding import Mesh
from jax.sharding import PartitionSpec as P

ITERS = 2
RADAR_TILE = ("radar_0", "radar_1", "tile_0", "tile_1")
RADAR = ("radar_0", "radar_1")
TILE = ("tile_0", "tile_1")
BACKGROUND_WEIGHT = 0.5
DIVERGENCE_WEIGHT = 1.0
STEP_LENGTH = 0.3
EPSILON = 1e-06


def padded_2(x, sides, width):
    edges = {}
    for axis, dim in sides:
        size, length = (lax.axis_size(axis), x.shape[dim])
        up = [(i, (i + 1) % size) for i in range(size - 1)]
        last = lax.slice_in_dim(x, length - width, length, axis=dim)
        first = lax.slice_in_dim(x, 0, width, axis=dim)
        edges[dim] = (
            lax.ppermute(last, axis, up),
            lax.ppermute(first, axis, [(b, a) for a, b in up]),
        )
    done = []
    for _, dim in sides:
        low, high = edges[dim]
        around = [(width, width) if d in done else (0, 0) for d in range(x.ndim)]
        x = jnp.concatenate([jnp.pad(low, around), x, jnp.pad(high, around)], axis=dim)
        done.append(dim)
    return x


def split_up(x, dim, length):
    before, after = (x.shape[:dim], x.shape[dim + 1 :])
    return jnp.moveaxis(x.reshape(*before, length, -1, *after), dim, 0)


def laid_out(tiles, dim):
    tiles = jnp.moveaxis(tiles, 0, dim)
    shape = tiles.shape
    return tiles.reshape(*shape[:dim], shape[dim] * shape[dim + 1], *shape[dim + 2 :])


def joined_exchange(x, axis, axes, splits, concats):
    sizes = [lax.axis_size(a) for a in axes]
    tiles = split_up(x, splits[0], sizes[0])
    tiles = jnp.moveaxis(split_up(tiles, splits[1] + 1, sizes[1]), 0, 1)
    inside = tiles.shape[2:]
    tiles = tiles.reshape(-1, *inside)
    tiles = lax.all_to_all(tiles, axis, split_axis=0, concat_axis=0, tiled=True)
    tiles = laid_out(tiles.reshape(*sizes, *inside), concats[0] + 1)
    return laid_out(tiles, concats[1])


def over_axes(x, axes):
    for axis in axes:
        x = lax.psum(x, axis)
    return x


def vertical_diff(values):
    padded = jnp.pad(values, ((0, 0), (1, 1), (0, 0)))
    return 0.5 * (padded[:, 2:, :] - padded[:, :-2, :])


def along_x(values):
    return 0.5 * (values[2:, :, 1:-1] - values[:-2, :, 1:-1])


def along_y(values):
    return 0.5 * (values[1:-1, :, 2:] - values[1:-1, :, :-2])


def along_z(values):
    return vertical_diff(values[1:-1, :, 1:-1])


def observe(cell_rows, weights, beam_rows, looked, alive_mask):
    projected = jnp.einsum("knc,ngc->nkg", cell_rows, weights, preferred_element_type=jnp.float32)
    beam_values = beam_rows.astype(jnp.float32)
    radial = jnp.sum(beam_values * projected, axis=1)
    misfit = alive_mask[:, None] * (radial - looked.astype(jnp.float32))
    adjoint = (beam_values * misfit[:, None, :]).astype(jnp.bfloat16)
    returned = jnp.einsum("nkg,ngc->knc", adjoint, weights, preferred_element_type=jnp.float32)
    return (0.5 * jnp.sum(misfit * misfit), returned)


def spread_faces(wind_field):
    faces = padded_2(wind_field[:2], ((RADAR, 3), (TILE, 1)), 1)
    spread = along_x(faces[0]) + along_y(faces[1]) + vertical_diff(wind_field[2])
    beside_all = padded_2(spread, ((RADAR, 2), (TILE, 0)), 1)
    push = jnp.stack([-along_x(beside_all), -along_y(beside_all), -vertical_diff(spread)])
    return (spread, push)


def shards(background, interp, beam, observed, cell_block, sweep_count):
    radar_count = lax.axis_size(RADAR)
    tile_count = lax.axis_size(TILE)
    devices = radar_count * tile_count
    width_x = background.shape[1]
    levels = background.shape[2]
    width_y = background.shape[3]
    slots = interp.shape[0] // devices
    gate_size = interp.shape[1]
    block_total = width_x * levels * width_y // gate_size
    total_cells = 3 * width_x * levels * width_y * devices
    total_gates = interp.shape[0] * devices * gate_size
    own_index = cell_block.reshape(devices, slots)
    own_alive = (
        jnp.arange(slots, dtype=jnp.int32)[None, :] < sweep_count.reshape(devices)[:, None]
    ).astype(jnp.int32)
    packed = jnp.stack([own_index, own_alive], 1)
    asked = lax.all_to_all(packed, RADAR_TILE, split_axis=0, concat_axis=0, tiled=True)
    asked_index = asked[:, 0, :].reshape(-1)
    local_alive = own_alive.reshape(-1).astype(jnp.float32)
    wind_field = background
    trace = []
    for step_index in range(ITERS):
        flat = wind_field.reshape(3, block_total, gate_size)
        empty = jnp.zeros((3, block_total, gate_size), jnp.float32)
        chosen = flat[:, asked_index, :].astype(jnp.bfloat16)
        arriving = joined_exchange(
            chosen.reshape(3, radar_count, tile_count, slots, gate_size),
            RADAR_TILE,
            (RADAR, TILE),
            (1, 2),
            (1, 2),
        )
        obs_cost, returned = observe(
            arriving.reshape(3, devices * slots, gate_size), interp, beam, observed, local_alive
        )
        landed = joined_exchange(
            returned.reshape(3, radar_count, tile_count, slots, gate_size),
            RADAR_TILE,
            (RADAR, TILE),
            (1, 2),
            (1, 2),
        )
        obs_cost, obs_flat = (
            obs_cost,
            empty.at[:, asked_index, :].add(landed.reshape(3, devices * slots, gate_size)),
        )
        obs_grad = obs_flat.reshape(wind_field.shape)
        spread, push = spread_faces(wind_field)
        offset = wind_field - background
        gradient = obs_grad + BACKGROUND_WEIGHT * offset + DIVERGENCE_WEIGHT * push
        local_cost = (
            obs_cost
            + 0.5 * BACKGROUND_WEIGHT * jnp.sum(offset * offset)
            + 0.5 * DIVERGENCE_WEIGHT * jnp.sum(spread * spread)
        )
        cost_sum, square_sum = (
            over_axes(local_cost, RADAR_TILE),
            over_axes(jnp.sum(gradient * gradient), RADAR_TILE),
        )
        scale = jnp.sqrt(square_sum / total_cells + EPSILON)
        wind_field = wind_field - STEP_LENGTH * gradient / scale
        trace.append(cost_sum / total_gates)
    faces = padded_2(wind_field, ((RADAR, 3), (TILE, 1)), 1)
    east_wind, north_wind, upward_wind = (faces[0], faces[1], faces[2])
    strain = jnp.stack(
        [
            along_x(east_wind),
            along_y(north_wind),
            along_z(upward_wind),
            0.5 * (along_y(east_wind) + along_x(north_wind)),
            0.5 * (along_z(east_wind) + along_x(upward_wind)),
            0.5 * (along_z(north_wind) + along_y(upward_wind)),
        ]
    )
    return (wind_field, strain, jnp.stack(trace))


def solution(mesh):
    torus = Mesh(mesh.devices.reshape(4, 2, 4, 4), ("radar_0", "radar_1", "tile_0", "tile_1"))
    in_specs = (
        P(None, TILE, None, RADAR),
        P(RADAR_TILE, None, None),
        P(RADAR_TILE, None, None),
        P(RADAR_TILE, None),
        P(RADAR_TILE),
        P(RADAR_TILE, None),
    )
    out_specs = (P(None, TILE, None, RADAR), P(None, TILE, None, RADAR), P())
    return jax.shard_map(
        shards, mesh=torus, in_specs=in_specs, out_specs=out_specs, check_vma=False
    )
```

profile of v0, /device:TPU:98, one launch (start us, length us, event | category | flops | bytes accessed | tf_op | source)
XLA Modules:
  0.0 330.2 jit_solution(9535569945727988790)
XLA Ops:
  0.7 2.4 fusion.83
  5.0 3.6 %collective-permute-start.2 = (f32[2,16,32,1]{3,2,1,0:T(8,128)}, f32[2,16,32,1]{3,2,1,0:T(8,128)}, u32[]{:S(2)}, u32[]{:S(2)}) collective-permute-start(f32[2,16,32,1]{3,2,1,0:T(8,128)} %get-tuple-element.44), channel_id=1, source_target_pairs={{16,0},{32,16},{48,32},{64,48},{80,64},{96,80},{112,96},{17,1},{33... | collective-permute-start | bytes 12296 | tf_op jit(solution)/shard_map/ppermute | solution.py:26
  8.7 2.1 collective-permute-start
  10.8 3.7 %collective-permute-start.3 = (f32[2,1,32,256]{3,2,1,0:T(8,128)S(1)}, f32[2,1,32,256]{3,2,1,0:T(8,128)S(1)}, u32[]{:S(2)}, u32[]{:S(2)}) collective-permute-start(f32[2,1,32,256]{3,2,1,0:T(8,128)S(1)} %get-tuple-element.46), channel_id=1, source_target_pairs={{1,0},{2,1},{3,2},{4,3},{5,4},{6,5},{7,6},{8,7},{9,8},{10,9},{11,1... | collective-permute-start | bytes 196616 | tf_op jit(solution)/shard_map/ppermute | solution.py:26
  15.6 9.8 %all-to-all-start = ((s32[128,2,2]{2,1,0:T(2,128)}), s32[128,2,2]{2,1,0:T(2,128)S(1)}, u32[]{:S(2)}, u32[]{:S(2)}) async-start(s32[128,2,2]{2,1,0:T(2,128)} %copy.39), calls=%async_computation | async-start | bytes 262144 | tf_op jit(solution)/shard_map/all_to_all | solution.py:117
  27.6 4.4 %all-to-all-done = s32[128,2,2]{2,1,0:T(2,128)S(1)} async-done(((s32[128,2,2]{2,1,0:T(2,128)}), s32[128,2,2]{2,1,0:T(2,128)S(1)}, u32[]{:S(2)}, u32[]{:S(2)}) %all-to-all-start) | async-done | bytes 2080 | tf_op jit(solution)/shard_map/all_to_all | solution.py:117
  32.3 2.2 gather_fusion
  35.4 7.7 %all-to-all-start.1 = ((bf16[128,3,1,1,2,128]{5,4,3,2,1,0:T(2,128)(2,1)}), bf16[128,3,1,1,2,128]{5,4,3,2,1,0:T(2,128)(2,1)S(1)}, u32[]{:S(2)}, u32[]{:S(2)}) async-start(bf16[128,3,1,1,2,128]{5,4,3,2,1,0:T(2,128)(2,1)} %bitcast.7), calls=%async_computation.1 | async-start | bytes 393216 | tf_op jit(solution)/shard_map/all_to_all | solution.py:54
  46.2 2.5 collective-permute-start.6
  48.7 5.5 %collective-permute-start.7 = (f32[1,32,256]{2,1,0:T(8,128)S(1)}, f32[1,32,256]{2,1,0:T(8,128)S(1)}, u32[]{:S(2)}, u32[]{:S(2)}) collective-permute-start(f32[1,32,256]{2,1,0:T(8,128)S(1)} %get-tuple-element.58), channel_id=1, source_target_pairs={{0,1},{1,2},{2,3},{3,4},{4,5},{5,6},{6,7},{7,8},{8,9},{9,10},{10,1... | collective-permute-start | bytes 98312 | tf_op jit(solution)/shard_map/ppermute | solution.py:25
  54.3 7.9 %fusion = f32[256,128]{1,0:T(8,128)S(1)} fusion(bf16[3,256,128]{2,0,1:T(4,128)(2,1)S(1)} %bitcast.151, bf16[256,128,128]{2,1,0:T(8,128)(2,1)} %param.7, bf16[256,3,128]{2,0,1:T(8,128)(2,1)S(1)} %copy-done.4), kind=kOutput, calls=%fused_computation.24 | convolution fusion | flops 25427968 | bytes 8912896 | tf_op jit(solution)/shard_map/knc,ngc->nkg/dot_general | solution.py:83
  62.9 5.6 %fusion.66 = f32[256,3,128]{2,1,0:T(4,128)S(1)} fusion(bf16[256,128,128]{2,1,0:T(8,128)(2,1)} %param.7, f32[256,128]{1,0:T(8,128)S(1)} %get-tuple-element.20, bf16[256,3,128]{2,0,1:T(8,128)(2,1)S(1)} %copy-done.4), kind=kOutput, calls=%fused_computation.144 | convolution fusion | flops 25460736 | bytes 9109504 | tf_op jit(solution)/shard_map/nkg,ngc->knc/dot_general | solution.py:88
  69.5 9.7 %all-to-all-start.2 = ((f32[128,3,1,1,2,128]{5,4,3,2,1,0:T(2,128)}), f32[128,3,1,1,2,128]{5,4,3,2,1,0:T(2,128)S(1)}, u32[]{:S(2)}, u32[]{:S(2)}) async-start(f32[128,3,1,1,2,128]{5,4,3,2,1,0:T(2,128)} %bitcast.18), calls=%async_computation.2 | async-start | bytes 786432 | tf_op jit(solution)/shard_map/all_to_all | solution.py:54
  79.4 2.1 collective-permute-start.4
  81.4 3.7 %collective-permute-start.5 = (f32[16,32,1]{2,1,0:T(8,128)S(1)}, f32[16,32,1]{2,1,0:T(8,128)S(1)}, u32[]{:S(2)}, u32[]{:S(2)}) collective-permute-start(f32[16,32,1]{2,1,0:T(8,128)S(1)} %get-tuple-element.59), channel_id=1, source_target_pairs={{16,0},{32,16},{48,32},{64,48},{80,64},{96,80},{112,96},{17,1},{33... | collective-permute-start | bytes 6152 | tf_op jit(solution)/shard_map/ppermute | solution.py:26
  90.9 8.3 %scatter_fusion = f32[3,1024,128]{2,0,1:T(4,128)S(1)} fusion(f32[3,1024,128]{2,0,1:T(4,128)S(1)} %broadcast.90.clone, s32[256]{0:T(256)S(1)} %bitcast.159, f32[256,3,128]{2,1,0:T(4,128)S(1)} %bitcast.147), kind=kCustom, calls=%fused_computation.2 | custom fusion | flops 98304 | bytes 1180672 | tf_op jit(solution)/shard_map/scatter-add | solution.py:145
  102.4 3.0 multiply_reduce_fusion.3
  105.4 9.3 %psum.112 = f32[]{:T(128)} all-reduce(f32[]{:T(128)} %multiply_reduce_fusion.3), channel_id=1, replica_groups=mesh['radar_0'=4,'radar_1'=2,'tile_0'=4,'tile_1'=4] {'radar_0'}, use_global_device_ids=true, to_apply=%region_3.4 | all-reduce | flops 1 | bytes 8 | tf_op jit(solution)/shard_map/psum | solution.py:61
  114.6 3.1 psum.113
  117.8 11.3 %psum.114 = f32[]{:T(128)} all-reduce(f32[]{:T(128)} %psum.113), channel_id=1, replica_groups=mesh['radar_0'=4,'radar_1'=2,'tile_0'=4,'tile_1'=4] {'tile_0'}, use_global_device_ids=true, to_apply=%region_5.6 | all-reduce | flops 1 | bytes 8 | tf_op jit(solution)/shard_map/psum | solution.py:61
  129.1 8.1 %psum.115 = f32[]{:T(128)} all-reduce(f32[]{:T(128)} %psum.114), channel_id=1, replica_groups=mesh['radar_0'=4,'radar_1'=2,'tile_0'=4,'tile_1'=4] {'tile_1'}, use_global_device_ids=true, to_apply=%region_6.7 | all-reduce | flops 1 | bytes 8 | tf_op jit(solution)/shard_map/psum | solution.py:61
  137.9 3.2 multiply_reduce_fusion.1
  144.7 2.4 collective-permute-start.9
  147.2 3.6 %collective-permute-start.11 = (f32[2,1,32,256]{3,2,1,0:T(8,128)}, f32[2,1,32,256]{3,2,1,0:T(8,128)}, u32[]{:S(2)}, u32[]{:S(2)}) collective-permute-start(f32[2,1,32,256]{3,2,1,0:T(8,128)} %get-tuple-element.42), channel_id=1, source_target_pairs={{1,0},{2,1},{3,2},{4,3},{5,4},{6,5},{7,6},{8,7},{9,8},{10,9},{11,1... | collective-permute-start | bytes 196616 | tf_op jit(solution)/shard_map/ppermute | solution.py:26
  150.7 4.4 %collective-permute-start.8 = (f32[2,1,32,256]{3,2,1,0:T(8,128)}, f32[2,1,32,256]{3,2,1,0:T(8,128)}, u32[]{:S(2)}, u32[]{:S(2)}) collective-permute-start(f32[2,1,32,256]{3,2,1,0:T(8,128)} %get-tuple-element.41), channel_id=1, source_target_pairs={{0,1},{1,2},{2,3},{3,4},{4,5},{5,6},{6,7},{7,8},{8,9},{9,10},{10,1... | collective-permute-start | bytes 196616 | tf_op jit(solution)/shard_map/ppermute | solution.py:25
  160.2 2.9 gather_fusion.1
  164.9 8.8 %all-to-all-start.3 = ((bf16[128,3,1,1,2,128]{5,4,3,2,1,0:T(2,128)(2,1)}), bf16[128,3,1,1,2,128]{5,4,3,2,1,0:T(2,128)(2,1)S(1)}, u32[]{:S(2)}, u32[]{:S(2)}) async-start(bf16[128,3,1,1,2,128]{5,4,3,2,1,0:T(2,128)(2,1)} %bitcast.157), calls=%async_computation.3 | async-start | bytes 393216 | tf_op jit(solution)/shard_map/all_to_all | solution.py:54
  173.8 2.3 select_maximum_fusion.2
  179.5 2.5 collective-permute-start.14
  182.0 5.7 %collective-permute-start.15 = (f32[1,32,256]{2,1,0:T(8,128)}, f32[1,32,256]{2,1,0:T(8,128)}, u32[]{:S(2)}, u32[]{:S(2)}) collective-permute-start(f32[1,32,256]{2,1,0:T(8,128)} %get-tuple-element.53), channel_id=1, source_target_pairs={{0,1},{1,2},{2,3},{3,4},{4,5},{5,6},{6,7},{7,8},{8,9},{9,10},{10,1... | collective-permute-start | bytes 98312 | tf_op jit(solution)/shard_map/ppermute | solution.py:25
  187.8 7.9 %fusion.1 = f32[256,128]{1,0:T(8,128)S(1)} fusion(bf16[3,256,128]{2,0,1:T(4,128)(2,1)S(1)} %bitcast.152, bf16[256,128,128]{2,1,0:T(8,128)(2,1)} %param.7, bf16[256,3,128]{2,0,1:T(8,128)(2,1)S(1)} %copy-done.4), kind=kOutput, calls=%fused_computation.25 | convolution fusion | flops 25427968 | bytes 8912896 | tf_op jit(solution)/shard_map/knc,ngc->nkg/dot_general | solution.py:83
  196.5 5.6 %fusion.64 = f32[256,3,128]{2,1,0:T(4,128)S(1)} fusion(bf16[256,128,128]{2,1,0:T(8,128)(2,1)} %param.7, f32[256,128]{1,0:T(8,128)S(1)} %get-tuple-element.25, bf16[256,3,128]{2,0,1:T(8,128)(2,1)S(1)} %copy-done.4), kind=kOutput, calls=%fused_computation.143 | convolution fusion | flops 25460736 | bytes 9109504 | tf_op jit(solution)/shard_map/nkg,ngc->knc/dot_general | solution.py:88
  203.1 9.7 %all-to-all-start.4 = ((f32[128,3,1,1,2,128]{5,4,3,2,1,0:T(2,128)}), f32[128,3,1,1,2,128]{5,4,3,2,1,0:T(2,128)S(1)}, u32[]{:S(2)}, u32[]{:S(2)}) async-start(f32[128,3,1,1,2,128]{5,4,3,2,1,0:T(2,128)} %bitcast.149), calls=%async_computation.4 | async-start | bytes 786432 | tf_op jit(solution)/shard_map/all_to_all | solution.py:54
  214.7 2.0 collective-permute-start.12
  216.8 3.5 %collective-permute-start.13 = (f32[16,32,1]{2,1,0:T(8,128)}, f32[16,32,1]{2,1,0:T(8,128)}, u32[]{:S(2)}, u32[]{:S(2)}) collective-permute-start(f32[16,32,1]{2,1,0:T(8,128)} %get-tuple-element.54), channel_id=1, source_target_pairs={{16,0},{32,16},{48,32},{64,48},{80,64},{96,80},{112,96},{17,1},{33... | collective-permute-start | bytes 6152 | tf_op jit(solution)/shard_map/ppermute | solution.py:26
  224.5 4.3 %fusion.50 = (f32[1,16,32,256]{3,2,1,0:T(8,128)}, f32[1,16,32,256]{3,2,1,0:T(8,128)}, f32[1,16,32,256]{3,2,1,0:T(8,128)}) fusion(f32[1,32,256]{2,1,0:T(8,128)} %collective-permute-done.15, f32[16,32,1]{2,1,0:T(8,128)} %collective-permute-done.13, f32[16,32,256]{2,1,0:T(8,128)} %copy-done.5, f32[16,32,1]{2,1,0:T(8,128)} %collective-permute-done.12, ...), kind=kLoop, calls=%fused_computation.106 | loop fusion | flops 3014656 | bytes 2166784 | tf_op jit(solution)/shard_map/stack | solution.py:96
  232.0 27.8 %scatter_fusion.1 = f32[3,1024,128]{2,0,1:T(4,128)} fusion(f32[3,1024,128]{2,0,1:T(4,128)} %broadcast.90, s32[256]{0:T(256)S(1)} %bitcast.160, f32[256,3,128]{2,1,0:T(4,128)} %bitcast.146), kind=kCustom, calls=%fused_computation.3 | custom fusion | flops 98304 | bytes 1180672 | tf_op jit(solution)/shard_map/scatter-add | solution.py:145
  259.7 2.8 copy.52
  262.6 2.7 reshape.195
  265.3 4.2 %multiply_reduce_fusion.2 = (f32[]{:T(128)}, f32[3,16,32,256]{3,2,1,0:T(8,128)}) fusion(f32[1,16,32,256]{3,2,1,0:T(8,128)} %get-tuple-element.51, f32[1,16,32,256]{3,2,1,0:T(8,128)} %get-tuple-element.48, f32[1,16,32,256]{3,2,1,0:T(8,128)} %get-tuple-element.47, f32[3,16,32,256]{3,2,1,0:T(8,128)} %reshape.195, f32[3,16,32,256]{3,2,1,0:T(8,128)S(1)} %get-tuple-element.23, ...), kind=kLoop, calls=%fused_computation.19 | loop fusion | flops 3145727 | bytes 7864324 | tf_op jit(solution)/shard_map/reduce_sum | solution.py:158
  269.4 9.3 %all-reduce.19 = (f32[]{:T(128)}, f32[]{:T(128)}, f32[]{:T(128)}) all-reduce(f32[]{:T(128)} %get-tuple-element.26, f32[]{:T(128)S(6)} %add.149, f32[]{:T(128)S(6)} %add.147), channel_id=1, replica_groups=mesh['radar_0'=4,'radar_1'=2,'tile_0'=4,'tile_1'=4] {'radar_0'}, use_global_device_ids=true, to_apply=%region_10.11 | all-reduce | flops 3 | bytes 24 | tf_op jit(solution)/shard_map/psum | solution.py:61
  278.7 3.1 all-reduce.20
  281.8 11.3 %all-reduce.18 = (f32[]{:T(128)}, f32[]{:T(128)}, f32[]{:T(128)}) all-reduce(f32[]{:T(128)} %get-tuple-element.14, f32[]{:T(128)} %get-tuple-element.15, f32[]{:T(128)} %get-tuple-element.16), channel_id=1, replica_groups=mesh['radar_0'=4,'radar_1'=2,'tile_0'=4,'tile_1'=4] {'tile_0'}, use_global_device_ids=true, to_apply=%region_12.13 | all-reduce | flops 3 | bytes 24 | tf_op jit(solution)/shard_map/psum | solution.py:61
  293.1 8.1 %all-reduce.17 = (f32[]{:T(128)}, f32[]{:T(128)}, f32[]{:T(128)}) all-reduce(f32[]{:T(128)} %get-tuple-element.8, f32[]{:T(128)} %get-tuple-element.9, f32[]{:T(128)} %get-tuple-element.10), channel_id=1, replica_groups=mesh['radar_0'=4,'radar_1'=2,'tile_0'=4,'tile_1'=4] {'tile_1'}, use_global_device_ids=true, to_apply=%region_13.14 | all-reduce | flops 3 | bytes 24 | tf_op jit(solution)/shard_map/psum | solution.py:61
  308.4 3.6 %collective-permute-start.18 = (f32[3,16,32,1]{2,1,3,0:T(8,128)S(1)}, f32[3,16,32,1]{2,1,3,0:T(8,128)}, u32[]{:S(2)}, u32[]{:S(2)}) collective-permute-start(f32[3,16,32,1]{2,1,3,0:T(8,128)S(1)} %copy.54), channel_id=1, source_target_pairs={{16,0},{32,16},{48,32},{64,48},{80,64},{96,80},{112,96},{17,1},{33... | collective-permute-start | bytes 18440 | tf_op jit(solution)/shard_map/ppermute | solution.py:26
  312.0 4.4 %collective-permute-start.16 = (f32[3,1,32,256]{3,2,1,0:T(8,128)S(1)}, f32[3,1,32,256]{3,2,1,0:T(8,128)S(1)}, u32[]{:S(2)}, u32[]{:S(2)}) collective-permute-start(f32[3,1,32,256]{3,2,1,0:T(8,128)S(1)} %get-tuple-element.37), channel_id=1, source_target_pairs={{0,1},{1,2},{2,3},{3,4},{4,5},{5,6},{6,7},{7,8},{8,9},{9,10},{10,1... | collective-permute-start | bytes 294920 | tf_op jit(solution)/shard_map/ppermute | solution.py:25
  316.5 2.2 collective-permute-start.19
  320.7 4.4 %collective-permute-done.19 = f32[3,1,32,256]{3,2,1,0:T(8,128)S(1)} collective-permute-done((f32[3,1,32,256]{3,2,1,0:T(8,128)S(1)}, f32[3,1,32,256]{3,2,1,0:T(8,128)S(1)}, u32[]{:S(2)}, u32[]{:S(2)}) %collective-permute-start.19) | collective-permute-done | bytes 98336 | tf_op jit(solution)/shard_map/ppermute | solution.py:26
  (117 shorter events, 54.0 us)
Async XLA Ops:
  0.6 8.0 %copy-start = (f32[3,16,32,256]{3,2,1,0:T(8,128)S(1)}, f32[3,16,32,256]{3,2,1,0:T(8,128)}, u32[]{:S(2)}) copy-start(f32[3,16,32,256]{3,2,1,0:T(8,128)} %param.6) | copy-start | bytes 4718596
  0.6 13.9 %copy-start.11 = (s32[1,128]{1,0:T(1,128)S(1)}, s32[1,128]{1,0:T(1,128)}, u32[]{:S(2)}) copy-start(s32[1,128]{1,0:T(1,128)} %param.11) | copy-start | bytes 1540
  0.7 14.0 %copy-start.12 = (s32[256]{0:T(256)S(1)}, s32[256]{0:T(256)}, u32[]{:S(2)}) copy-start(s32[256]{0:T(256)} %param.10) | copy-start | bytes 3076
  3.1 40.0 %collective-permute-start.1 = (f32[2,16,32,1]{3,2,1,0:T(8,128)}, f32[2,16,32,1]{3,2,1,0:T(8,128)}, u32[]{:S(2)}, u32[]{:S(2)}) collective-permute-start(f32[2,16,32,1]{3,2,1,0:T(8,128)} %get-tuple-element.43), channel_id=1, source_target_pairs={{0,16},{16,32},{32,48},{48,64},{64,80},{80,96},{96,112},{1,17},{17... | collective-permute-start | bytes 12296 | tf_op jit(solution)/shard_map/ppermute | solution.py:25
  5.0 38.1 %collective-permute-start.2 = (f32[2,16,32,1]{3,2,1,0:T(8,128)}, f32[2,16,32,1]{3,2,1,0:T(8,128)}, u32[]{:S(2)}, u32[]{:S(2)}) collective-permute-start(f32[2,16,32,1]{3,2,1,0:T(8,128)} %get-tuple-element.44), channel_id=1, source_target_pairs={{16,0},{32,16},{48,32},{64,48},{80,64},{96,80},{112,96},{17,1},{33... | collective-permute-start | bytes 12296 | tf_op jit(solution)/shard_map/ppermute | solution.py:26
  8.7 34.4 %collective-permute-start = (f32[2,1,32,256]{3,2,1,0:T(8,128)S(1)}, f32[2,1,32,256]{3,2,1,0:T(8,128)S(1)}, u32[]{:S(2)}, u32[]{:S(2)}) collective-permute-start(f32[2,1,32,256]{3,2,1,0:T(8,128)S(1)} %get-tuple-element.45), channel_id=1, source_target_pairs={{0,1},{1,2},{2,3},{3,4},{4,5},{5,6},{6,7},{7,8},{8,9},{9,10},{10,1... | collective-permute-start | bytes 196616 | tf_op jit(solution)/shard_map/ppermute | solution.py:25
  10.8 32.3 %collective-permute-start.3 = (f32[2,1,32,256]{3,2,1,0:T(8,128)S(1)}, f32[2,1,32,256]{3,2,1,0:T(8,128)S(1)}, u32[]{:S(2)}, u32[]{:S(2)}) collective-permute-start(f32[2,1,32,256]{3,2,1,0:T(8,128)S(1)} %get-tuple-element.46), channel_id=1, source_target_pairs={{1,0},{2,1},{3,2},{4,3},{5,4},{6,5},{7,6},{8,7},{9,8},{10,9},{11,1... | collective-permute-start | bytes 196616 | tf_op jit(solution)/shard_map/ppermute | solution.py:26
  15.6 16.4 %all-to-all-start = ((s32[128,2,2]{2,1,0:T(2,128)}), s32[128,2,2]{2,1,0:T(2,128)S(1)}, u32[]{:S(2)}, u32[]{:S(2)}) async-start(s32[128,2,2]{2,1,0:T(2,128)} %copy.39), calls=%async_computation | async-start | bytes 262144 | tf_op jit(solution)/shard_map/all_to_all | solution.py:117
  25.8 17.3 %slice-start = ((f32[3,16,32,256]{3,2,1,0:T(8,128)}), f32[2,16,32,256]{3,2,1,0:T(8,128)S(1)}, s32[]{:S(2)}) async-start(f32[3,16,32,256]{3,2,1,0:T(8,128)} %param.6), calls=%async_computation.5 | async-start | bytes 2097152 | tf_op jit(solution)/shard_map/slice | solution.py:93
  35.4 18.8 %all-to-all-start.1 = ((bf16[128,3,1,1,2,128]{5,4,3,2,1,0:T(2,128)(2,1)}), bf16[128,3,1,1,2,128]{5,4,3,2,1,0:T(2,128)(2,1)S(1)}, u32[]{:S(2)}, u32[]{:S(2)}) async-start(bf16[128,3,1,1,2,128]{5,4,3,2,1,0:T(2,128)(2,1)} %bitcast.7), calls=%async_computation.1 | async-start | bytes 393216 | tf_op jit(solution)/shard_map/all_to_all | solution.py:54
  45.1 9.2 %copy-start.4 = (bf16[256,3,128]{2,0,1:T(8,128)(2,1)S(1)}, bf16[256,3,128]{2,0,1:T(8,128)(2,1)}, u32[]{:S(2)}) copy-start(bf16[256,3,128]{2,0,1:T(8,128)(2,1)} %param.8) | copy-start | bytes 589828
  46.2 42.6 %collective-permute-start.6 = (f32[1,32,256]{2,1,0:T(8,128)S(1)}, f32[1,32,256]{2,1,0:T(8,128)S(1)}, u32[]{:S(2)}, u32[]{:S(2)}) collective-permute-start(f32[1,32,256]{2,1,0:T(8,128)S(1)} %get-tuple-element.57), channel_id=1, source_target_pairs={{1,0},{2,1},{3,2},{4,3},{5,4},{6,5},{7,6},{8,7},{9,8},{10,9},{11,1... | collective-permute-start | bytes 98312 | tf_op jit(solution)/shard_map/ppermute | solution.py:26
  48.7 40.1 %collective-permute-start.7 = (f32[1,32,256]{2,1,0:T(8,128)S(1)}, f32[1,32,256]{2,1,0:T(8,128)S(1)}, u32[]{:S(2)}, u32[]{:S(2)}) collective-permute-start(f32[1,32,256]{2,1,0:T(8,128)S(1)} %get-tuple-element.58), channel_id=1, source_target_pairs={{0,1},{1,2},{2,3},{3,4},{4,5},{5,6},{6,7},{7,8},{8,9},{9,10},{10,1... | collective-permute-start | bytes 98312 | tf_op jit(solution)/shard_map/ppermute | solution.py:25
  54.3 7.9 %copy-start.8 = (bf16[256,128]{1,0:T(8,128)(2,1)S(1)}, bf16[256,128]{1,0:T(8,128)(2,1)}, u32[]{:S(2)}) copy-start(bf16[256,128]{1,0:T(8,128)(2,1)} %param.9) | copy-start | bytes 196612
  69.5 21.0 %all-to-all-start.2 = ((f32[128,3,1,1,2,128]{5,4,3,2,1,0:T(2,128)}), f32[128,3,1,1,2,128]{5,4,3,2,1,0:T(2,128)S(1)}, u32[]{:S(2)}, u32[]{:S(2)}) async-start(f32[128,3,1,1,2,128]{5,4,3,2,1,0:T(2,128)} %bitcast.18), calls=%async_computation.2 | async-start | bytes 786432 | tf_op jit(solution)/shard_map/all_to_all | solution.py:54
  79.4 7.8 %collective-permute-start.4 = (f32[16,32,1]{2,1,0:T(8,128)S(1)}, f32[16,32,1]{2,1,0:T(8,128)S(1)}, u32[]{:S(2)}, u32[]{:S(2)}) collective-permute-start(f32[16,32,1]{2,1,0:T(8,128)S(1)} %get-tuple-element.60), channel_id=1, source_target_pairs={{0,16},{16,32},{32,48},{48,64},{64,80},{80,96},{96,112},{1,17},{17... | collective-permute-start | bytes 6152 | tf_op jit(solution)/shard_map/ppermute | solution.py:25
  81.4 7.4 %collective-permute-start.5 = (f32[16,32,1]{2,1,0:T(8,128)S(1)}, f32[16,32,1]{2,1,0:T(8,128)S(1)}, u32[]{:S(2)}, u32[]{:S(2)}) collective-permute-start(f32[16,32,1]{2,1,0:T(8,128)S(1)} %get-tuple-element.59), channel_id=1, source_target_pairs={{16,0},{32,16},{48,32},{64,48},{80,64},{96,80},{112,96},{17,1},{33... | collective-permute-start | bytes 6152 | tf_op jit(solution)/shard_map/ppermute | solution.py:26
  100.5 1.9 copy-start.1
  102.3 3.0 copy-start.3
  142.8 30.9 %collective-permute-start.10 = (f32[2,16,32,1]{3,2,1,0:T(8,128)}, f32[2,16,32,1]{3,2,1,0:T(8,128)}, u32[]{:S(2)}, u32[]{:S(2)}) collective-permute-start(f32[2,16,32,1]{3,2,1,0:T(8,128)} %get-tuple-element.40), channel_id=1, source_target_pairs={{16,0},{32,16},{48,32},{64,48},{80,64},{96,80},{112,96},{17,1},{33... | collective-permute-start | bytes 12296 | tf_op jit(solution)/shard_map/ppermute | solution.py:26
  144.7 29.0 %collective-permute-start.9 = (f32[2,16,32,1]{3,2,1,0:T(8,128)}, f32[2,16,32,1]{3,2,1,0:T(8,128)}, u32[]{:S(2)}, u32[]{:S(2)}) collective-permute-start(f32[2,16,32,1]{3,2,1,0:T(8,128)} %get-tuple-element.39), channel_id=1, source_target_pairs={{0,16},{16,32},{32,48},{48,64},{64,80},{80,96},{96,112},{1,17},{17... | collective-permute-start | bytes 12296 | tf_op jit(solution)/shard_map/ppermute | solution.py:25
  147.2 26.6 %collective-permute-start.11 = (f32[2,1,32,256]{3,2,1,0:T(8,128)}, f32[2,1,32,256]{3,2,1,0:T(8,128)}, u32[]{:S(2)}, u32[]{:S(2)}) collective-permute-start(f32[2,1,32,256]{3,2,1,0:T(8,128)} %get-tuple-element.42), channel_id=1, source_target_pairs={{1,0},{2,1},{3,2},{4,3},{5,4},{6,5},{7,6},{8,7},{9,8},{10,9},{11,1... | collective-permute-start | bytes 196616 | tf_op jit(solution)/shard_map/ppermute | solution.py:26
  150.7 23.0 %collective-permute-start.8 = (f32[2,1,32,256]{3,2,1,0:T(8,128)}, f32[2,1,32,256]{3,2,1,0:T(8,128)}, u32[]{:S(2)}, u32[]{:S(2)}) collective-permute-start(f32[2,1,32,256]{3,2,1,0:T(8,128)} %get-tuple-element.41), channel_id=1, source_target_pairs={{0,1},{1,2},{2,3},{3,4},{4,5},{5,6},{6,7},{7,8},{8,9},{9,10},{10,1... | collective-permute-start | bytes 196616 | tf_op jit(solution)/shard_map/ppermute | solution.py:25
  157.0 1.5 copy-start.6
  164.9 22.8 %all-to-all-start.3 = ((bf16[128,3,1,1,2,128]{5,4,3,2,1,0:T(2,128)(2,1)}), bf16[128,3,1,1,2,128]{5,4,3,2,1,0:T(2,128)(2,1)S(1)}, u32[]{:S(2)}, u32[]{:S(2)}) async-start(bf16[128,3,1,1,2,128]{5,4,3,2,1,0:T(2,128)(2,1)} %bitcast.157), calls=%async_computation.3 | async-start | bytes 393216 | tf_op jit(solution)/shard_map/all_to_all | solution.py:54
  176.0 1.0 copy-start.7
  178.1 0.8 copy-start.5
  179.5 45.0 %collective-permute-start.14 = (f32[1,32,256]{2,1,0:T(8,128)}, f32[1,32,256]{2,1,0:T(8,128)}, u32[]{:S(2)}, u32[]{:S(2)}) collective-permute-start(f32[1,32,256]{2,1,0:T(8,128)} %get-tuple-element.52), channel_id=1, source_target_pairs={{1,0},{2,1},{3,2},{4,3},{5,4},{6,5},{7,6},{8,7},{9,8},{10,9},{11,1... | collective-permute-start | bytes 98312 | tf_op jit(solution)/shard_map/ppermute | solution.py:26
  182.0 42.5 %collective-permute-start.15 = (f32[1,32,256]{2,1,0:T(8,128)}, f32[1,32,256]{2,1,0:T(8,128)}, u32[]{:S(2)}, u32[]{:S(2)}) collective-permute-start(f32[1,32,256]{2,1,0:T(8,128)} %get-tuple-element.53), channel_id=1, source_target_pairs={{0,1},{1,2},{2,3},{3,4},{4,5},{5,6},{6,7},{7,8},{8,9},{9,10},{10,1... | collective-permute-start | bytes 98312 | tf_op jit(solution)/shard_map/ppermute | solution.py:25
  187.8 7.9 %copy-start.9 = (bf16[256,128]{1,0:T(8,128)(2,1)S(1)}, bf16[256,128]{1,0:T(8,128)(2,1)}, u32[]{:S(2)}) copy-start(bf16[256,128]{1,0:T(8,128)(2,1)} %param.9) | copy-start | bytes 196612
  203.1 26.4 %all-to-all-start.4 = ((f32[128,3,1,1,2,128]{5,4,3,2,1,0:T(2,128)}), f32[128,3,1,1,2,128]{5,4,3,2,1,0:T(2,128)S(1)}, u32[]{:S(2)}, u32[]{:S(2)}) async-start(f32[128,3,1,1,2,128]{5,4,3,2,1,0:T(2,128)} %bitcast.149), calls=%async_computation.4 | async-start | bytes 786432 | tf_op jit(solution)/shard_map/all_to_all | solution.py:54
  214.7 8.6 %collective-permute-start.12 = (f32[16,32,1]{2,1,0:T(8,128)}, f32[16,32,1]{2,1,0:T(8,128)}, u32[]{:S(2)}, u32[]{:S(2)}) collective-permute-start(f32[16,32,1]{2,1,0:T(8,128)} %get-tuple-element.55), channel_id=1, source_target_pairs={{0,16},{16,32},{32,48},{48,64},{64,80},{80,96},{96,112},{1,17},{17... | collective-permute-start | bytes 6152 | tf_op jit(solution)/shard_map/ppermute | solution.py:25
  216.8 7.7 %collective-permute-start.13 = (f32[16,32,1]{2,1,0:T(8,128)}, f32[16,32,1]{2,1,0:T(8,128)}, u32[]{:S(2)}, u32[]{:S(2)}) collective-permute-start(f32[16,32,1]{2,1,0:T(8,128)} %get-tuple-element.54), channel_id=1, source_target_pairs={{16,0},{32,16},{48,32},{64,48},{80,64},{96,80},{112,96},{17,1},{33... | collective-permute-start | bytes 6152 | tf_op jit(solution)/shard_map/ppermute | solution.py:26
  303.6 21.5 %copy-start.2 = (f32[3,16,32,256]{3,2,1,0:T(8,128)}, f32[3,16,32,256]{3,2,1,0:T(8,128)S(1)}, u32[]{:S(2)}) copy-start(f32[3,16,32,256]{3,2,1,0:T(8,128)S(1)} %divide_subtract_fusion) | copy-start | bytes 4718596
  306.1 13.1 %collective-permute-start.17 = (f32[3,16,32,1]{2,1,3,0:T(8,128)}, f32[3,16,32,1]{2,1,3,0:T(8,128)S(1)}, u32[]{:S(2)}, u32[]{:S(2)}) collective-permute-start(f32[3,16,32,1]{2,1,3,0:T(8,128)} %copy.53), channel_id=1, source_target_pairs={{0,16},{16,32},{32,48},{48,64},{64,80},{80,96},{96,112},{1,17},{17... | collective-permute-start | bytes 18440 | tf_op jit(solution)/shard_map/ppermute | solution.py:25
  308.4 11.2 %collective-permute-start.18 = (f32[3,16,32,1]{2,1,3,0:T(8,128)S(1)}, f32[3,16,32,1]{2,1,3,0:T(8,128)}, u32[]{:S(2)}, u32[]{:S(2)}) collective-permute-start(f32[3,16,32,1]{2,1,3,0:T(8,128)S(1)} %copy.54), channel_id=1, source_target_pairs={{16,0},{32,16},{48,32},{64,48},{80,64},{96,80},{112,96},{17,1},{33... | collective-permute-start | bytes 18440 | tf_op jit(solution)/shard_map/ppermute | solution.py:26
  312.0 8.7 %collective-permute-start.16 = (f32[3,1,32,256]{3,2,1,0:T(8,128)S(1)}, f32[3,1,32,256]{3,2,1,0:T(8,128)S(1)}, u32[]{:S(2)}, u32[]{:S(2)}) collective-permute-start(f32[3,1,32,256]{3,2,1,0:T(8,128)S(1)} %get-tuple-element.37), channel_id=1, source_target_pairs={{0,1},{1,2},{2,3},{3,4},{4,5},{5,6},{6,7},{7,8},{8,9},{9,10},{10,1... | collective-permute-start | bytes 294920 | tf_op jit(solution)/shard_map/ppermute | solution.py:25
  316.5 8.6 %collective-permute-start.19 = (f32[3,1,32,256]{3,2,1,0:T(8,128)S(1)}, f32[3,1,32,256]{3,2,1,0:T(8,128)S(1)}, u32[]{:S(2)}, u32[]{:S(2)}) collective-permute-start(f32[3,1,32,256]{3,2,1,0:T(8,128)S(1)} %get-tuple-element.38), channel_id=1, source_target_pairs={{1,0},{2,1},{3,2},{4,3},{5,4},{6,5},{7,6},{8,7},{9,8},{10,9},{11,1... | collective-permute-start | bytes 294920 | tf_op jit(solution)/shard_map/ppermute | solution.py:26
  328.6 1.7 copy-start.10
where the time goes:
time: 333 us; the launch traced here: 330 us
  starting transfers between devices  109 us (33%)
  other arithmetic  65.3 us (20%)
  blocking collectives  63.6 us (19%)
  local copies, waits for them, and re-layouts  44.1 us (13%)
  matrix products  27 us (8%)
  waiting for transfers between devices  13.7 us (4%)
  between operations  7.62 us (2%)
    psum x8, blocking collectives, over_axes(): x = lax.psum(x, axis)  63.6 us
    scatter-add x2, other arithmetic, shards(): empty.at[:, asked_index, :]  36.1 us
    all_to_all x4, starting transfers between devices, joined_exchange(): tiles = lax.all_to_all(tiles, axis, split_axis=0, concat_axis=0, tiled=True)  36 us
    ppermute x10, starting transfers between devices, padded_2(): lax.ppermute(last, axis, up)  32.4 us
    ppermute x10, starting transfers between devices, padded_2(): lax.ppermute(first, axis, [(b, a) for a, b in up])  30.8 us
    dot_general x2, matrix products, observe(): jnp.einsum('knc,ngc->nkg', cell_rows, weights, preferred_element_type=jnp...  15.7 us
    dot_general x2, matrix products, observe(): jnp.einsum('nkg,ngc->knc', adjoint, weights, preferred_element_type=jnp.f...  11.3 us
    all_to_all x1, starting transfers between devices, shards(): lax.all_to_all(packed, RADAR_TILE, split_axis=0, concat_axis=0, tiled=True)  9.84 us
  transfers between devices with their start and end apart: 25, of which 5 were waited for; matrix products, arithmetic and copies ran while one was open for 19% of the time, Pallas kernels for 0%

commit v1 on v0

--- a/solution.py
+++ b/solution.py
@@ -58,7 +58,8 @@
 
 def over_axes(x, axes):
     for axis in axes:
-        x = lax.psum(x, axis)
+        parts = lax.all_gather(x, axis)
+        x = jnp.sum(parts, axis=0)
     return x
 
 

time: 333 us -> 360 us (1.081)
  local copies, waits for them, and re-layouts: 44.1 us -> 67 us
  other arithmetic: 65.3 us -> 75.3 us
  blocking collectives: 63.6 us -> 58.1 us
    psum x8 -> x0, blocking collectives: 63.6 us -> none  [over_axes(): x = lax.psum(x, axis)]
    unnamed x0 -> x8, blocking collectives: none -> 58.1 us
    unnamed x26 -> x70, local copies, waits for them, and re-layouts: 3.87 us -> 26.8 us
    reduce_sum x0 -> x16, other arithmetic: none -> 9.96 us  [over_axes(): x = jnp.sum(parts, axis=0)]
  transfers between devices with their start and end apart: 25 -> 25, of which waited for: 5 -> 5; matrix products, arithmetic and copies ran while one was open for 19% -> 18% of each run, Pallas kernels for 0% -> 0%
where the time goes in v1:
time: 360 us; the launch traced here: 357 us
  starting transfers between devices  109 us (30%)
  other arithmetic  75.3 us (21%)
  local copies, waits for them, and re-layouts  67 us (19%)
  blocking collectives  58.1 us (16%)
  matrix products  27 us (8%)
  waiting for transfers between devices  12.3 us (3%)
  between operations  7.93 us (2%)
    unnamed x8, blocking collectives  58.1 us
    scatter-add x2, other arithmetic, shards(): empty.at[:, asked_index, :]  36.1 us
    all_to_all x4, starting transfers between devices, joined_exchange(): tiles = lax.all_to_all(tiles, axis, split_axis=0, concat_axis=0, tiled=True)  36 us
    ppermute x10, starting transfers between devices, padded_2(): lax.ppermute(last, axis, up)  32.4 us
    ppermute x10, starting transfers between devices, padded_2(): lax.ppermute(first, axis, [(b, a) for a, b in up])  30.8 us
    unnamed x70, local copies, waits for them, and re-layouts  26.8 us
    dot_general x2, matrix products, observe(): jnp.einsum('knc,ngc->nkg', cell_rows, weights, preferred_element_type=jnp...  15.7 us
    dot_general x2, matrix products, observe(): jnp.einsum('nkg,ngc->knc', adjoint, weights, preferred_element_type=jnp.f...  11.3 us
  transfers between devices with their start and end apart: 25, of which 5 were waited for; matrix products, arithmetic and copies ran while one was open for 18% of the time, Pallas kernels for 0%

profile of v1, /device:TPU:98, one launch (start us, length us, event | category | flops | bytes accessed | tf_op | source)
XLA Modules:
  0.0 356.6 jit_solution(417610631183465954)
XLA Ops:
  0.7 2.4 fusion.83
  5.0 3.6 %collective-permute-start.2 = (f32[2,16,32,1]{3,2,1,0:T(8,128)}, f32[2,16,32,1]{3,2,1,0:T(8,128)}, u32[]{:S(2)}, u32[]{:S(2)}) collective-permute-start(f32[2,16,32,1]{3,2,1,0:T(8,128)} %get-tuple-element.44), channel_id=1, source_target_pairs={{16,0},{32,16},{48,32},{64,48},{80,64},{96,80},{112,96},{17,1},{33... | collective-permute-start | bytes 12296 | tf_op jit(solution)/shard_map/ppermute | solution.py:26
  8.7 2.1 collective-permute-start
  10.8 3.7 %collective-permute-start.3 = (f32[2,1,32,256]{3,2,1,0:T(8,128)S(1)}, f32[2,1,32,256]{3,2,1,0:T(8,128)S(1)}, u32[]{:S(2)}, u32[]{:S(2)}) collective-permute-start(f32[2,1,32,256]{3,2,1,0:T(8,128)S(1)} %get-tuple-element.46), channel_id=1, source_target_pairs={{1,0},{2,1},{3,2},{4,3},{5,4},{6,5},{7,6},{8,7},{9,8},{10,9},{11,1... | collective-permute-start | bytes 196616 | tf_op jit(solution)/shard_map/ppermute | solution.py:26
  15.6 9.8 %all-to-all-start = ((s32[128,2,2]{2,1,0:T(2,128)}), s32[128,2,2]{2,1,0:T(2,128)S(1)}, u32[]{:S(2)}, u32[]{:S(2)}) async-start(s32[128,2,2]{2,1,0:T(2,128)} %copy.39), calls=%async_computation | async-start | bytes 262144 | tf_op jit(solution)/shard_map/all_to_all | solution.py:118
  27.6 4.4 %all-to-all-done = s32[128,2,2]{2,1,0:T(2,128)S(1)} async-done(((s32[128,2,2]{2,1,0:T(2,128)}), s32[128,2,2]{2,1,0:T(2,128)S(1)}, u32[]{:S(2)}, u32[]{:S(2)}) %all-to-all-start) | async-done | bytes 2080 | tf_op jit(solution)/shard_map/all_to_all | solution.py:118
  32.3 2.2 gather_fusion
  35.4 7.7 %all-to-all-start.1 = ((bf16[128,3,1,1,2,128]{5,4,3,2,1,0:T(2,128)(2,1)}), bf16[128,3,1,1,2,128]{5,4,3,2,1,0:T(2,128)(2,1)S(1)}, u32[]{:S(2)}, u32[]{:S(2)}) async-start(bf16[128,3,1,1,2,128]{5,4,3,2,1,0:T(2,128)(2,1)} %bitcast.7), calls=%async_computation.1 | async-start | bytes 393216 | tf_op jit(solution)/shard_map/all_to_all | solution.py:54
  46.2 2.5 collective-permute-start.6
  48.7 5.5 %collective-permute-start.7 = (f32[1,32,256]{2,1,0:T(8,128)S(1)}, f32[1,32,256]{2,1,0:T(8,128)S(1)}, u32[]{:S(2)}, u32[]{:S(2)}) collective-permute-start(f32[1,32,256]{2,1,0:T(8,128)S(1)} %get-tuple-element.58), channel_id=1, source_target_pairs={{0,1},{1,2},{2,3},{3,4},{4,5},{5,6},{6,7},{7,8},{8,9},{9,10},{10,1... | collective-permute-start | bytes 98312 | tf_op jit(solution)/shard_map/ppermute | solution.py:25
  54.3 7.9 %fusion = f32[256,128]{1,0:T(8,128)S(1)} fusion(bf16[3,256,128]{2,0,1:T(4,128)(2,1)S(1)} %bitcast.171, bf16[256,128,128]{2,1,0:T(8,128)(2,1)} %param.7, bf16[256,3,128]{2,0,1:T(8,128)(2,1)S(1)} %copy-done.4), kind=kOutput, calls=%fused_computation.24 | convolution fusion | flops 25427968 | bytes 8912896 | tf_op jit(solution)/shard_map/knc,ngc->nkg/dot_general | solution.py:84
  62.8 5.6 %fusion.66 = f32[256,3,128]{2,1,0:T(4,128)S(1)} fusion(bf16[256,128,128]{2,1,0:T(8,128)(2,1)} %param.7, f32[256,128]{1,0:T(8,128)S(1)} %get-tuple-element.20, bf16[256,3,128]{2,0,1:T(8,128)(2,1)S(1)} %copy-done.4), kind=kOutput, calls=%fused_computation.144 | convolution fusion | flops 25460736 | bytes 9109504 | tf_op jit(solution)/shard_map/nkg,ngc->knc/dot_general | solution.py:89
  69.4 9.7 %all-to-all-start.2 = ((f32[128,3,1,1,2,128]{5,4,3,2,1,0:T(2,128)}), f32[128,3,1,1,2,128]{5,4,3,2,1,0:T(2,128)S(1)}, u32[]{:S(2)}, u32[]{:S(2)}) async-start(f32[128,3,1,1,2,128]{5,4,3,2,1,0:T(2,128)} %bitcast.18), calls=%async_computation.2 | async-start | bytes 786432 | tf_op jit(solution)/shard_map/all_to_all | solution.py:54
  79.3 2.1 collective-permute-start.4
  81.4 3.7 %collective-permute-start.5 = (f32[16,32,1]{2,1,0:T(8,128)S(1)}, f32[16,32,1]{2,1,0:T(8,128)S(1)}, u32[]{:S(2)}, u32[]{:S(2)}) collective-permute-start(f32[16,32,1]{2,1,0:T(8,128)S(1)} %get-tuple-element.59), channel_id=1, source_target_pairs={{16,0},{32,16},{48,32},{64,48},{80,64},{96,80},{112,96},{17,1},{33... | collective-permute-start | bytes 6152 | tf_op jit(solution)/shard_map/ppermute | solution.py:26
  90.9 8.3 %scatter_fusion = f32[3,1024,128]{2,0,1:T(4,128)S(1)} fusion(f32[3,1024,128]{2,0,1:T(4,128)S(1)} %broadcast.90.clone, s32[256]{0:T(256)S(1)} %bitcast.179, f32[256,3,128]{2,1,0:T(4,128)S(1)} %bitcast.167), kind=kCustom, calls=%fused_computation.2 | custom fusion | flops 98304 | bytes 1180672 | tf_op jit(solution)/shard_map/scatter-add | solution.py:146
  102.4 3.0 multiply_reduce_fusion.3
  107.2 8.6 %all-reduce.17 = f32[4]{0:T(128)S(1)} all-reduce(f32[4]{0:T(128)S(1)} %dynamic-update-slice), channel_id=1, replica_groups=mesh['radar_0'=4,'radar_1'=2,'tile_0'=4,'tile_1'=4] {'radar_0'}, use_global_device_ids=true, to_apply=%add.17 | all-reduce | flops 4 | bytes 32
  118.6 2.4 all-reduce.18
  123.6 10.6 %all-reduce.19 = f32[4]{0:T(128)S(1)} all-reduce(f32[4]{0:T(128)S(1)} %dynamic-update-slice.2), channel_id=1, replica_groups=mesh['radar_0'=4,'radar_1'=2,'tile_0'=4,'tile_1'=4] {'tile_0'}, use_global_device_ids=true, to_apply=%add.19 | all-reduce | flops 4 | bytes 32
  136.2 7.4 %all-reduce.20 = f32[4]{0:T(128)S(1)} all-reduce(f32[4]{0:T(128)S(1)} %dynamic-update-slice.3), channel_id=1, replica_groups=mesh['radar_0'=4,'radar_1'=2,'tile_0'=4,'tile_1'=4] {'tile_1'}, use_global_device_ids=true, to_apply=%add.20 | all-reduce | flops 4 | bytes 32
  145.1 3.2 multiply_reduce_fusion.1
  152.0 2.4 collective-permute-start.9
  154.4 3.6 %collective-permute-start.11 = (f32[2,1,32,256]{3,2,1,0:T(8,128)}, f32[2,1,32,256]{3,2,1,0:T(8,128)}, u32[]{:S(2)}, u32[]{:S(2)}) collective-permute-start(f32[2,1,32,256]{3,2,1,0:T(8,128)} %get-tuple-element.42), channel_id=1, source_target_pairs={{1,0},{2,1},{3,2},{4,3},{5,4},{6,5},{7,6},{8,7},{9,8},{10,9},{11,1... | collective-permute-start | bytes 196616 | tf_op jit(solution)/shard_map/ppermute | solution.py:26
  158.0 4.4 %collective-permute-start.8 = (f32[2,1,32,256]{3,2,1,0:T(8,128)}, f32[2,1,32,256]{3,2,1,0:T(8,128)}, u32[]{:S(2)}, u32[]{:S(2)}) collective-permute-start(f32[2,1,32,256]{3,2,1,0:T(8,128)} %get-tuple-element.41), channel_id=1, source_target_pairs={{0,1},{1,2},{2,3},{3,4},{4,5},{5,6},{6,7},{7,8},{8,9},{9,10},{10,1... | collective-permute-start | bytes 196616 | tf_op jit(solution)/shard_map/ppermute | solution.py:25
  167.4 2.9 gather_fusion.1
  172.1 8.8 %all-to-all-start.3 = ((bf16[128,3,1,1,2,128]{5,4,3,2,1,0:T(2,128)(2,1)}), bf16[128,3,1,1,2,128]{5,4,3,2,1,0:T(2,128)(2,1)S(1)}, u32[]{:S(2)}, u32[]{:S(2)}) async-start(bf16[128,3,1,1,2,128]{5,4,3,2,1,0:T(2,128)(2,1)} %bitcast.177), calls=%async_computation.3 | async-start | bytes 393216 | tf_op jit(solution)/shard_map/all_to_all | solution.py:54
  181.0 2.3 select_maximum_fusion.2
  186.8 2.5 collective-permute-start.14
  189.3 5.7 %collective-permute-start.15 = (f32[1,32,256]{2,1,0:T(8,128)}, f32[1,32,256]{2,1,0:T(8,128)}, u32[]{:S(2)}, u32[]{:S(2)}) collective-permute-start(f32[1,32,256]{2,1,0:T(8,128)} %get-tuple-element.53), channel_id=1, source_target_pairs={{0,1},{1,2},{2,3},{3,4},{4,5},{5,6},{6,7},{7,8},{8,9},{9,10},{10,1... | collective-permute-start | bytes 98312 | tf_op jit(solution)/shard_map/ppermute | solution.py:25
  195.1 7.9 %fusion.1 = f32[256,128]{1,0:T(8,128)S(1)} fusion(bf16[3,256,128]{2,0,1:T(4,128)(2,1)S(1)} %bitcast.172, bf16[256,128,128]{2,1,0:T(8,128)(2,1)} %param.7, bf16[256,3,128]{2,0,1:T(8,128)(2,1)S(1)} %copy-done.4), kind=kOutput, calls=%fused_computation.25 | convolution fusion | flops 25427968 | bytes 8912896 | tf_op jit(solution)/shard_map/knc,ngc->nkg/dot_general | solution.py:84
  203.8 5.6 %fusion.64 = f32[256,3,128]{2,1,0:T(4,128)S(1)} fusion(bf16[256,128,128]{2,1,0:T(8,128)(2,1)} %param.7, f32[256,128]{1,0:T(8,128)S(1)} %get-tuple-element.25, bf16[256,3,128]{2,0,1:T(8,128)(2,1)S(1)} %copy-done.4), kind=kOutput, calls=%fused_computation.143 | convolution fusion | flops 25460736 | bytes 9109504 | tf_op jit(solution)/shard_map/nkg,ngc->knc/dot_general | solution.py:89
  210.4 9.7 %all-to-all-start.4 = ((f32[128,3,1,1,2,128]{5,4,3,2,1,0:T(2,128)}), f32[128,3,1,1,2,128]{5,4,3,2,1,0:T(2,128)S(1)}, u32[]{:S(2)}, u32[]{:S(2)}) async-start(f32[128,3,1,1,2,128]{5,4,3,2,1,0:T(2,128)} %bitcast.169), calls=%async_computation.4 | async-start | bytes 786432 | tf_op jit(solution)/shard_map/all_to_all | solution.py:54
  222.0 2.0 collective-permute-start.12
  224.1 3.5 collective-permute-start.13
  231.8 4.4 %fusion.50 = (f32[1,16,32,256]{3,2,1,0:T(8,128)}, f32[1,16,32,256]{3,2,1,0:T(8,128)}, f32[1,16,32,256]{3,2,1,0:T(8,128)}) fusion(f32[1,32,256]{2,1,0:T(8,128)} %collective-permute-done.15, f32[16,32,1]{2,1,0:T(8,128)} %collective-permute-done.13, f32[16,32,256]{2,1,0:T(8,128)} %copy-done.5, f32[16,32,1]{2,1,0:T(8,128)} %collective-permute-done.12, ...), kind=kLoop, calls=%fused_computation.106 | loop fusion | flops 3014656 | bytes 2166784 | tf_op jit(solution)/shard_map/stack | solution.py:97
  240.0 27.8 %scatter_fusion.1 = f32[3,1024,128]{2,0,1:T(4,128)} fusion(f32[3,1024,128]{2,0,1:T(4,128)} %broadcast.90, s32[256]{0:T(256)S(1)} %bitcast.180, f32[256,3,128]{2,1,0:T(4,128)} %bitcast.166), kind=kCustom, calls=%fused_computation.3 | custom fusion | flops 98304 | bytes 1180672 | tf_op jit(solution)/shard_map/scatter-add | solution.py:146
  267.7 2.8 copy.52
  270.6 2.7 reshape.195
  273.2 4.2 %multiply_reduce_fusion.2 = (f32[]{:T(128)}, f32[3,16,32,256]{3,2,1,0:T(8,128)}) fusion(f32[1,16,32,256]{3,2,1,0:T(8,128)} %get-tuple-element.51, f32[1,16,32,256]{3,2,1,0:T(8,128)} %get-tuple-element.48, f32[1,16,32,256]{3,2,1,0:T(8,128)} %get-tuple-element.47, f32[3,16,32,256]{3,2,1,0:T(8,128)} %reshape.195, f32[3,16,32,256]{3,2,1,0:T(8,128)S(1)} %get-tuple-element.23, ...), kind=kLoop, calls=%fused_computation.19 | loop fusion | flops 3145727 | bytes 7864324 | tf_op jit(solution)/shard_map/reduce_sum | solution.py:159
  278.7 8.6 %all-reduce.35 = (f32[4]{0:T(128)S(1)}, f32[4]{0:T(128)S(1)}, f32[4]{0:T(128)S(1)}) all-reduce(f32[4]{0:T(128)S(1)} %dynamic-update-slice.4, f32[4]{0:T(128)S(1)} %dynamic-update-slice.12, f32[4]{0:T(128)S(1)} %dynamic-update-slice.8), channel_id=1, replica_groups=mesh['radar_0'=4,'radar_1'=2,'tile_0'=4,'tile_1'=4] {'radar_0'}, use_global_device_ids=true, to_apply=%add.21 | all-reduce | flops 12 | bytes 96
  293.2 2.4 all-reduce.36
  301.8 10.6 %all-reduce.34 = (f32[4]{0:T(128)S(1)}, f32[4]{0:T(128)S(1)}, f32[4]{0:T(128)S(1)}) all-reduce(f32[4]{0:T(128)S(1)} %dynamic-update-slice.6, f32[4]{0:T(128)S(1)} %dynamic-update-slice.14, f32[4]{0:T(128)S(1)} %dynamic-update-slice.10), channel_id=1, replica_groups=mesh['radar_0'=4,'radar_1'=2,'tile_0'=4,'tile_1'=4] {'tile_0'}, use_global_device_ids=true, to_apply=%add.23 | all-reduce | flops 12 | bytes 96
  318.2 7.4 %all-reduce.33 = (f32[4]{0:T(128)S(1)}, f32[4]{0:T(128)S(1)}, f32[4]{0:T(128)S(1)}) all-reduce(f32[4]{0:T(128)S(1)} %dynamic-update-slice.7, f32[4]{0:T(128)S(1)} %dynamic-update-slice.15, f32[4]{0:T(128)S(1)} %dynamic-update-slice.11), channel_id=1, replica_groups=mesh['radar_0'=4,'radar_1'=2,'tile_0'=4,'tile_1'=4] {'tile_1'}, use_global_device_ids=true, to_apply=%add.24 | all-reduce | flops 12 | bytes 96
  334.8 3.6 %collective-permute-start.18 = (f32[3,16,32,1]{2,1,3,0:T(8,128)S(1)}, f32[3,16,32,1]{2,1,3,0:T(8,128)}, u32[]{:S(2)}, u32[]{:S(2)}) collective-permute-start(f32[3,16,32,1]{2,1,3,0:T(8,128)S(1)} %copy.54), channel_id=1, source_target_pairs={{16,0},{32,16},{48,32},{64,48},{80,64},{96,80},{112,96},{17,1},{33... | collective-permute-start | bytes 18440 | tf_op jit(solution)/shard_map/ppermute | solution.py:26
  338.5 4.4 %collective-permute-start.16 = (f32[3,1,32,256]{3,2,1,0:T(8,128)S(1)}, f32[3,1,32,256]{3,2,1,0:T(8,128)S(1)}, u32[]{:S(2)}, u32[]{:S(2)}) collective-permute-start(f32[3,1,32,256]{3,2,1,0:T(8,128)S(1)} %get-tuple-element.37), channel_id=1, source_target_pairs={{0,1},{1,2},{2,3},{3,4},{4,5},{5,6},{6,7},{7,8},{8,9},{9,10},{10,1... | collective-permute-start | bytes 294920 | tf_op jit(solution)/shard_map/ppermute | solution.py:25
  342.9 2.2 collective-permute-start.19
  347.1 4.4 %collective-permute-done.19 = f32[3,1,32,256]{3,2,1,0:T(8,128)S(1)} collective-permute-done((f32[3,1,32,256]{3,2,1,0:T(8,128)S(1)}, f32[3,1,32,256]{3,2,1,0:T(8,128)S(1)}, u32[]{:S(2)}, u32[]{:S(2)}) %collective-permute-start.19) | collective-permute-done | bytes 98336 | tf_op jit(solution)/shard_map/ppermute | solution.py:26
  (177 shorter events, 85.5 us)
Async XLA Ops:
  0.6 8.0 %copy-start = (f32[3,16,32,256]{3,2,1,0:T(8,128)S(1)}, f32[3,16,32,256]{3,2,1,0:T(8,128)}, u32[]{:S(2)}) copy-start(f32[3,16,32,256]{3,2,1,0:T(8,128)} %param.6) | copy-start | bytes 4718596
  0.6 13.9 %copy-start.11 = (s32[1,128]{1,0:T(1,128)S(1)}, s32[1,128]{1,0:T(1,128)}, u32[]{:S(2)}) copy-start(s32[1,128]{1,0:T(1,128)} %param.11) | copy-start | bytes 1540
  0.7 14.0 %copy-start.12 = (s32[256]{0:T(256)S(1)}, s32[256]{0:T(256)}, u32[]{:S(2)}) copy-start(s32[256]{0:T(256)} %param.10) | copy-start | bytes 3076
  3.1 40.0 %collective-permute-start.1 = (f32[2,16,32,1]{3,2,1,0:T(8,128)}, f32[2,16,32,1]{3,2,1,0:T(8,128)}, u32[]{:S(2)}, u32[]{:S(2)}) collective-permute-start(f32[2,16,32,1]{3,2,1,0:T(8,128)} %get-tuple-element.43), channel_id=1, source_target_pairs={{0,16},{16,32},{32,48},{48,64},{64,80},{80,96},{96,112},{1,17},{17... | collective-permute-start | bytes 12296 | tf_op jit(solution)/shard_map/ppermute | solution.py:25
  5.0 38.0 %collective-permute-start.2 = (f32[2,16,32,1]{3,2,1,0:T(8,128)}, f32[2,16,32,1]{3,2,1,0:T(8,128)}, u32[]{:S(2)}, u32[]{:S(2)}) collective-permute-start(f32[2,16,32,1]{3,2,1,0:T(8,128)} %get-tuple-element.44), channel_id=1, source_target_pairs={{16,0},{32,16},{48,32},{64,48},{80,64},{96,80},{112,96},{17,1},{33... | collective-permute-start | bytes 12296 | tf_op jit(solution)/shard_map/ppermute | solution.py:26
  8.7 34.4 %collective-permute-start = (f32[2,1,32,256]{3,2,1,0:T(8,128)S(1)}, f32[2,1,32,256]{3,2,1,0:T(8,128)S(1)}, u32[]{:S(2)}, u32[]{:S(2)}) collective-permute-start(f32[2,1,32,256]{3,2,1,0:T(8,128)S(1)} %get-tuple-element.45), channel_id=1, source_target_pairs={{0,1},{1,2},{2,3},{3,4},{4,5},{5,6},{6,7},{7,8},{8,9},{9,10},{10,1... | collective-permute-start | bytes 196616 | tf_op jit(solution)/shard_map/ppermute | solution.py:25
  10.8 32.3 %collective-permute-start.3 = (f32[2,1,32,256]{3,2,1,0:T(8,128)S(1)}, f32[2,1,32,256]{3,2,1,0:T(8,128)S(1)}, u32[]{:S(2)}, u32[]{:S(2)}) collective-permute-start(f32[2,1,32,256]{3,2,1,0:T(8,128)S(1)} %get-tuple-element.46), channel_id=1, source_target_pairs={{1,0},{2,1},{3,2},{4,3},{5,4},{6,5},{7,6},{8,7},{9,8},{10,9},{11,1... | collective-permute-start | bytes 196616 | tf_op jit(solution)/shard_map/ppermute | solution.py:26
  15.6 16.4 %all-to-all-start = ((s32[128,2,2]{2,1,0:T(2,128)}), s32[128,2,2]{2,1,0:T(2,128)S(1)}, u32[]{:S(2)}, u32[]{:S(2)}) async-start(s32[128,2,2]{2,1,0:T(2,128)} %copy.39), calls=%async_computation | async-start | bytes 262144 | tf_op jit(solution)/shard_map/all_to_all | solution.py:118
  25.8 17.3 %slice-start = ((f32[3,16,32,256]{3,2,1,0:T(8,128)}), f32[2,16,32,256]{3,2,1,0:T(8,128)S(1)}, s32[]{:S(2)}) async-start(f32[3,16,32,256]{3,2,1,0:T(8,128)} %param.6), calls=%async_computation.5 | async-start | bytes 2097152 | tf_op jit(solution)/shard_map/slice | solution.py:94
  35.4 18.8 %all-to-all-start.1 = ((bf16[128,3,1,1,2,128]{5,4,3,2,1,0:T(2,128)(2,1)}), bf16[128,3,1,1,2,128]{5,4,3,2,1,0:T(2,128)(2,1)S(1)}, u32[]{:S(2)}, u32[]{:S(2)}) async-start(bf16[128,3,1,1,2,128]{5,4,3,2,1,0:T(2,128)(2,1)} %bitcast.7), calls=%async_computation.1 | async-start | bytes 393216 | tf_op jit(solution)/shard_map/all_to_all | solution.py:54
  45.1 9.2 %copy-start.4 = (bf16[256,3,128]{2,0,1:T(8,128)(2,1)S(1)}, bf16[256,3,128]{2,0,1:T(8,128)(2,1)}, u32[]{:S(2)}) copy-start(bf16[256,3,128]{2,0,1:T(8,128)(2,1)} %param.8) | copy-start | bytes 589828
  46.2 42.6 %collective-permute-start.6 = (f32[1,32,256]{2,1,0:T(8,128)S(1)}, f32[1,32,256]{2,1,0:T(8,128)S(1)}, u32[]{:S(2)}, u32[]{:S(2)}) collective-permute-start(f32[1,32,256]{2,1,0:T(8,128)S(1)} %get-tuple-element.57), channel_id=1, source_target_pairs={{1,0},{2,1},{3,2},{4,3},{5,4},{6,5},{7,6},{8,7},{9,8},{10,9},{11,1... | collective-permute-start | bytes 98312 | tf_op jit(solution)/shard_map/ppermute | solution.py:26
  48.7 40.1 %collective-permute-start.7 = (f32[1,32,256]{2,1,0:T(8,128)S(1)}, f32[1,32,256]{2,1,0:T(8,128)S(1)}, u32[]{:S(2)}, u32[]{:S(2)}) collective-permute-start(f32[1,32,256]{2,1,0:T(8,128)S(1)} %get-tuple-element.58), channel_id=1, source_target_pairs={{0,1},{1,2},{2,3},{3,4},{4,5},{5,6},{6,7},{7,8},{8,9},{9,10},{10,1... | collective-permute-start | bytes 98312 | tf_op jit(solution)/shard_map/ppermute | solution.py:25
  54.3 7.9 %copy-start.8 = (bf16[256,128]{1,0:T(8,128)(2,1)S(1)}, bf16[256,128]{1,0:T(8,128)(2,1)}, u32[]{:S(2)}) copy-start(bf16[256,128]{1,0:T(8,128)(2,1)} %param.9) | copy-start | bytes 196612
  68.5 16.6 %copy-start.16 = (u32[128]{0:T(128)S(1)}, u32[128]{0:T(128)}, u32[]{:S(2)}) copy-start(u32[128]{0:T(128)} %constant.67) | copy-start | bytes 1540
  69.4 21.0 %all-to-all-start.2 = ((f32[128,3,1,1,2,128]{5,4,3,2,1,0:T(2,128)}), f32[128,3,1,1,2,128]{5,4,3,2,1,0:T(2,128)S(1)}, u32[]{:S(2)}, u32[]{:S(2)}) async-start(f32[128,3,1,1,2,128]{5,4,3,2,1,0:T(2,128)} %bitcast.18), calls=%async_computation.2 | async-start | bytes 786432 | tf_op jit(solution)/shard_map/all_to_all | solution.py:54
  79.3 7.8 %collective-permute-start.4 = (f32[16,32,1]{2,1,0:T(8,128)S(1)}, f32[16,32,1]{2,1,0:T(8,128)S(1)}, u32[]{:S(2)}, u32[]{:S(2)}) collective-permute-start(f32[16,32,1]{2,1,0:T(8,128)S(1)} %get-tuple-element.60), channel_id=1, source_target_pairs={{0,16},{16,32},{32,48},{48,64},{64,80},{80,96},{96,112},{1,17},{17... | collective-permute-start | bytes 6152 | tf_op jit(solution)/shard_map/ppermute | solution.py:25
  81.4 7.4 %collective-permute-start.5 = (f32[16,32,1]{2,1,0:T(8,128)S(1)}, f32[16,32,1]{2,1,0:T(8,128)S(1)}, u32[]{:S(2)}, u32[]{:S(2)}) collective-permute-start(f32[16,32,1]{2,1,0:T(8,128)S(1)} %get-tuple-element.59), channel_id=1, source_target_pairs={{16,0},{32,16},{48,32},{64,48},{80,64},{96,80},{112,96},{17,1},{33... | collective-permute-start | bytes 6152 | tf_op jit(solution)/shard_map/ppermute | solution.py:26
  100.5 1.9 copy-start.1
  102.3 3.0 copy-start.3
  102.4 4.3 %copy-start.15 = (u32[128]{0:T(128)S(1)}, u32[128]{0:T(128)}, u32[]{:S(2)}) copy-start(u32[128]{0:T(128)} %constant.72) | copy-start | bytes 1540
  102.4 15.5 %copy-start.14 = (u32[128]{0:T(128)S(1)}, u32[128]{0:T(128)}, u32[]{:S(2)}) copy-start(u32[128]{0:T(128)} %constant.77) | copy-start | bytes 1540
  102.4 20.6 %copy-start.13 = (u32[128]{0:T(128)S(1)}, u32[128]{0:T(128)}, u32[]{:S(2)}) copy-start(u32[128]{0:T(128)} %constant.82) | copy-start | bytes 1540
  150.1 30.9 %collective-permute-start.10 = (f32[2,16,32,1]{3,2,1,0:T(8,128)}, f32[2,16,32,1]{3,2,1,0:T(8,128)}, u32[]{:S(2)}, u32[]{:S(2)}) collective-permute-start(f32[2,16,32,1]{3,2,1,0:T(8,128)} %get-tuple-element.40), channel_id=1, source_target_pairs={{16,0},{32,16},{48,32},{64,48},{80,64},{96,80},{112,96},{17,1},{33... | collective-permute-start | bytes 12296 | tf_op jit(solution)/shard_map/ppermute | solution.py:26
  152.0 29.0 %collective-permute-start.9 = (f32[2,16,32,1]{3,2,1,0:T(8,128)}, f32[2,16,32,1]{3,2,1,0:T(8,128)}, u32[]{:S(2)}, u32[]{:S(2)}) collective-permute-start(f32[2,16,32,1]{3,2,1,0:T(8,128)} %get-tuple-element.39), channel_id=1, source_target_pairs={{0,16},{16,32},{32,48},{48,64},{64,80},{80,96},{96,112},{1,17},{17... | collective-permute-start | bytes 12296 | tf_op jit(solution)/shard_map/ppermute | solution.py:25
  154.4 26.6 %collective-permute-start.11 = (f32[2,1,32,256]{3,2,1,0:T(8,128)}, f32[2,1,32,256]{3,2,1,0:T(8,128)}, u32[]{:S(2)}, u32[]{:S(2)}) collective-permute-start(f32[2,1,32,256]{3,2,1,0:T(8,128)} %get-tuple-element.42), channel_id=1, source_target_pairs={{1,0},{2,1},{3,2},{4,3},{5,4},{6,5},{7,6},{8,7},{9,8},{10,9},{11,1... | collective-permute-start | bytes 196616 | tf_op jit(solution)/shard_map/ppermute | solution.py:26
  158.0 23.0 %collective-permute-start.8 = (f32[2,1,32,256]{3,2,1,0:T(8,128)}, f32[2,1,32,256]{3,2,1,0:T(8,128)}, u32[]{:S(2)}, u32[]{:S(2)}) collective-permute-start(f32[2,1,32,256]{3,2,1,0:T(8,128)} %get-tuple-element.41), channel_id=1, source_target_pairs={{0,1},{1,2},{2,3},{3,4},{4,5},{5,6},{6,7},{7,8},{8,9},{9,10},{10,1... | collective-permute-start | bytes 196616 | tf_op jit(solution)/shard_map/ppermute | solution.py:25
  164.3 1.5 copy-start.6
  172.1 22.9 %all-to-all-start.3 = ((bf16[128,3,1,1,2,128]{5,4,3,2,1,0:T(2,128)(2,1)}), bf16[128,3,1,1,2,128]{5,4,3,2,1,0:T(2,128)(2,1)S(1)}, u32[]{:S(2)}, u32[]{:S(2)}) async-start(bf16[128,3,1,1,2,128]{5,4,3,2,1,0:T(2,128)(2,1)} %bitcast.177), calls=%async_computation.3 | async-start | bytes 393216 | tf_op jit(solution)/shard_map/all_to_all | solution.py:54
  183.3 1.0 copy-start.7
  185.4 0.8 copy-start.5
  186.8 44.9 %collective-permute-start.14 = (f32[1,32,256]{2,1,0:T(8,128)}, f32[1,32,256]{2,1,0:T(8,128)}, u32[]{:S(2)}, u32[]{:S(2)}) collective-permute-start(f32[1,32,256]{2,1,0:T(8,128)} %get-tuple-element.52), channel_id=1, source_target_pairs={{1,0},{2,1},{3,2},{4,3},{5,4},{6,5},{7,6},{8,7},{9,8},{10,9},{11,1... | collective-permute-start | bytes 98312 | tf_op jit(solution)/shard_map/ppermute | solution.py:26
  189.3 42.4 %collective-permute-start.15 = (f32[1,32,256]{2,1,0:T(8,128)}, f32[1,32,256]{2,1,0:T(8,128)}, u32[]{:S(2)}, u32[]{:S(2)}) collective-permute-start(f32[1,32,256]{2,1,0:T(8,128)} %get-tuple-element.53), channel_id=1, source_target_pairs={{0,1},{1,2},{2,3},{3,4},{4,5},{5,6},{6,7},{7,8},{8,9},{9,10},{10,1... | collective-permute-start | bytes 98312 | tf_op jit(solution)/shard_map/ppermute | solution.py:25
  195.1 7.9 %copy-start.9 = (bf16[256,128]{1,0:T(8,128)(2,1)S(1)}, bf16[256,128]{1,0:T(8,128)(2,1)}, u32[]{:S(2)}) copy-start(bf16[256,128]{1,0:T(8,128)(2,1)} %param.9) | copy-start | bytes 196612
  210.4 27.1 %all-to-all-start.4 = ((f32[128,3,1,1,2,128]{5,4,3,2,1,0:T(2,128)}), f32[128,3,1,1,2,128]{5,4,3,2,1,0:T(2,128)S(1)}, u32[]{:S(2)}, u32[]{:S(2)}) async-start(f32[128,3,1,1,2,128]{5,4,3,2,1,0:T(2,128)} %bitcast.169), calls=%async_computation.4 | async-start | bytes 786432 | tf_op jit(solution)/shard_map/all_to_all | solution.py:54
  222.0 9.4 %collective-permute-start.12 = (f32[16,32,1]{2,1,0:T(8,128)}, f32[16,32,1]{2,1,0:T(8,128)}, u32[]{:S(2)}, u32[]{:S(2)}) collective-permute-start(f32[16,32,1]{2,1,0:T(8,128)} %get-tuple-element.55), channel_id=1, source_target_pairs={{0,16},{16,32},{32,48},{48,64},{64,80},{80,96},{96,112},{1,17},{17... | collective-permute-start | bytes 6152 | tf_op jit(solution)/shard_map/ppermute | solution.py:25
  224.1 7.7 %collective-permute-start.13 = (f32[16,32,1]{2,1,0:T(8,128)}, f32[16,32,1]{2,1,0:T(8,128)}, u32[]{:S(2)}, u32[]{:S(2)}) collective-permute-start(f32[16,32,1]{2,1,0:T(8,128)} %get-tuple-element.54), channel_id=1, source_target_pairs={{16,0},{32,16},{48,32},{64,48},{80,64},{96,80},{112,96},{17,1},{33... | collective-permute-start | bytes 6152 | tf_op jit(solution)/shard_map/ppermute | solution.py:26
  328.7 22.8 %copy-start.2 = (f32[3,16,32,256]{3,2,1,0:T(8,128)}, f32[3,16,32,256]{3,2,1,0:T(8,128)S(1)}, u32[]{:S(2)}) copy-start(f32[3,16,32,256]{3,2,1,0:T(8,128)S(1)} %divide_subtract_fusion) | copy-start | bytes 4718596
  332.6 13.1 %collective-permute-start.17 = (f32[3,16,32,1]{2,1,3,0:T(8,128)}, f32[3,16,32,1]{2,1,3,0:T(8,128)S(1)}, u32[]{:S(2)}, u32[]{:S(2)}) collective-permute-start(f32[3,16,32,1]{2,1,3,0:T(8,128)} %copy.53), channel_id=1, source_target_pairs={{0,16},{16,32},{32,48},{48,64},{64,80},{80,96},{96,112},{1,17},{17... | collective-permute-start | bytes 18440 | tf_op jit(solution)/shard_map/ppermute | solution.py:25
  334.8 11.2 %collective-permute-start.18 = (f32[3,16,32,1]{2,1,3,0:T(8,128)S(1)}, f32[3,16,32,1]{2,1,3,0:T(8,128)}, u32[]{:S(2)}, u32[]{:S(2)}) collective-permute-start(f32[3,16,32,1]{2,1,3,0:T(8,128)S(1)} %copy.54), channel_id=1, source_target_pairs={{16,0},{32,16},{48,32},{64,48},{80,64},{96,80},{112,96},{17,1},{33... | collective-permute-start | bytes 18440 | tf_op jit(solution)/shard_map/ppermute | solution.py:26
  338.5 8.7 %collective-permute-start.16 = (f32[3,1,32,256]{3,2,1,0:T(8,128)S(1)}, f32[3,1,32,256]{3,2,1,0:T(8,128)S(1)}, u32[]{:S(2)}, u32[]{:S(2)}) collective-permute-start(f32[3,1,32,256]{3,2,1,0:T(8,128)S(1)} %get-tuple-element.37), channel_id=1, source_target_pairs={{0,1},{1,2},{2,3},{3,4},{4,5},{5,6},{6,7},{7,8},{8,9},{9,10},{10,1... | collective-permute-start | bytes 294920 | tf_op jit(solution)/shard_map/ppermute | solution.py:25
  342.9 8.6 %collective-permute-start.19 = (f32[3,1,32,256]{3,2,1,0:T(8,128)S(1)}, f32[3,1,32,256]{3,2,1,0:T(8,128)S(1)}, u32[]{:S(2)}, u32[]{:S(2)}) collective-permute-start(f32[3,1,32,256]{3,2,1,0:T(8,128)S(1)} %get-tuple-element.38), channel_id=1, source_target_pairs={{1,0},{2,1},{3,2},{4,3},{5,4},{6,5},{7,6},{8,7},{9,8},{10,9},{11,1... | collective-permute-start | bytes 294920 | tf_op jit(solution)/shard_map/ppermute | solution.py:26
  355.0 1.7 copy-start.10
